TPU v7x, 512 devices: a whole 4x8x8 slice. The times are simulated.
512 devices in a mesh: seq: 64 (over x, y, core), expert: 8 (over z).
Axes of the slice: x: 4, y: 8, z: 8, core: 2. Of those that a mesh axis runs over, the one named last changes fastest.
Arguments:
- new_q: bfloat16 [64, 4, 1024], P('expert'), may hold values from -12 to 12
- new_k: bfloat16 [64, 4, 1024], P('expert'), may hold values from -12 to 12
- new_v: bfloat16 [64, 4, 1024], P('expert'), may hold values from -6 to 6
- k_cache: bfloat16 [8, 256, 128, 1024], P('expert', 'seq'), may hold values from -8 to 8
- v_cache: bfloat16 [8, 256, 128, 1024], P('expert', 'seq'), may hold values from -6 to 6
- lengths: int32 [64], P('expert'), may hold values from 4097 to 16384, as said below
- prompt_group: int32 [64], P('expert'), may hold values from 0 to 15, as said below
- prefix_table: int32 [16, 32], P('expert'), may hold values from 0 to 255, as said below
- page_table: int32 [64, 96], P('expert'), may hold values from -1 to 255, as said below
- rel_bucket: int32 [16388], replicated, may hold values from 0 to 31, as said below
- bias_table: float32 [32, 16], replicated, may hold values from -8 to 8
- hidden_in: bfloat16 [64, 4, 1024], P('expert', None, 'seq'), may hold values from -600 to 600
- out_proj: bfloat16 [1024, 1024], P(None, 'seq'), may hold values from -0.1875 to 0.1875
- norm_gain: float32 [1024], P('seq'), may hold values from 0.1 to 1.9
- router_w: float32 [1024, 16], P('seq'), may hold values from -0.1875 to 0.1875
- expert_ids: int32 [64, 4, 2], P('expert'), may hold values from 0 to 15, all different within a row; in each aligned block of 32 rows (0 to 31, 32 to 63, ..., all dimensions but the last counted through in order) at most 8 rows name the same one
- w_in: bfloat16 [16, 1024, 2, 2816], P('expert', None, None, 'seq'), may hold values from -0.1875 to 0.1875
- w_down: bfloat16 [16, 2816, 1024], P('expert', 'seq'), may hold values from -0.109375 to 0.109375
Outputs:
- attn_out: bfloat16 [64, 4, 1024], P('expert', None, 'seq')
- moe_out: bfloat16 [64, 4, 1024], P('expert', None, 'seq')
Inputs may be any that keep to these rules, and one draw needn't show every extreme that they name: `lengths`: at least 4097; in every block of 8 requests one request has exactly 16384. `prompt_group`: the groups of block b are b * 2 to b * 2 + 1, each holding 8 // 2 requests of that block. `prefix_table`: pages of the pool of the group's block. Entry j is -1 exactly when j * 128 is at least the request's own tokens, lengths - 4096. Within one block no pool page appears twice across prefix_table and page_table. `rel_bucket`: equal to the distance below 16; never falls as the distance grows. `expert_ids`: in the 32 rows of one block no expert is named more than 8 times.
All inputs are finite; a program needn't handle non-finite values.
Results may differ from a plain program's by a relative error of at most 0.014.
Values may be sent and summed in bfloat16 or wider, within the bound.
No kernel may reach another device: no remote copies, remote signals or barrier semaphores. Data moves between devices by JAX's collectives and lax.ppermute only.
A program may use at most 64 MiB of HBM per device.

v0:
```python
import math

import jax
import jax.numpy as jnp
from jax import lax
from jax.sharding import PartitionSpec as P

MOST = 8


neg_big = -1e30
eps_norm = 1e-06


def body(
    new_q,
    new_k,
    new_v,
    k_cache,
    v_cache,
    lengths,
    prompt_group,
    prefix_table,
    page_table,
    rel_bucket,
    bias_table,
    hidden_in,
    out_proj,
    norm_gain,
    router_w,
    expert_ids,
    w_in,
    w_down,
):
    req_count, step_count, model_width = new_q.shape
    bucket_count, head_count = bias_table.shape
    head_size = model_width // head_count
    pages_here = k_cache.shape[1]
    page_len = k_cache.shape[2]
    dist_limit = rel_bucket.shape[0]
    group_rows = prefix_table.shape[0]
    expert_here = w_in.shape[0]
    local_width = out_proj.shape[1]
    top_count = expert_ids.shape[2]
    seq_index = lax.axis_index("seq")
    pool_index = lax.axis_index("expert")
    expert_total = lax.axis_size("expert") * expert_here
    local_group = prompt_group - pool_index * group_rows
    group_hit = (local_group[:, None] == jnp.arange(group_rows, dtype=jnp.int32)[None, :]).astype(
        jnp.int32
    )
    prefix_rows = jnp.sum(group_hit[:, :, None] * prefix_table[None, :, :], axis=1)
    full_table = jnp.concatenate([prefix_rows, page_table], axis=1)
    page_ids = seq_index * pages_here + jnp.arange(pages_here, dtype=jnp.int32)
    matches = full_table[:, :, None] == page_ids[None, None, :]
    logical = jnp.sum(
        jnp.where(matches, jnp.arange(full_table.shape[1], dtype=jnp.int32)[None, :, None], 0),
        axis=1,
    )
    present = jnp.any(matches, axis=1)
    within = jnp.arange(page_len, dtype=jnp.int32)
    key_grid = logical[:, :, None] * page_len + within[None, None, :]
    usable = (present[:, :, None] & (key_grid < lengths[:, None, None])).reshape(req_count, -1)
    key_pos = key_grid.reshape(req_count, -1)
    query_pos = lengths[:, None] + jnp.arange(step_count, dtype=jnp.int32)[None, :]
    distance = jnp.clip(query_pos[:, :, None] - key_pos[:, None, :], 0, dist_limit - 1)
    buckets = rel_bucket[distance]
    onehot = (buckets[..., None] == jnp.arange(bucket_count, dtype=jnp.int32)).astype(jnp.float32)
    pos_bias = jnp.einsum("rskb,bh->rshk", onehot, bias_table, precision=lax.Precision.HIGHEST)
    queries = new_q.reshape(req_count, step_count, head_count, head_size)
    keys_here = k_cache[0].reshape(-1, head_count, head_size)
    values_here = v_cache[0].reshape(-1, head_count, head_size)
    scaling = 1.0 / math.sqrt(head_size)
    scores = (
        jnp.einsum("rshd,khd->rshk", queries, keys_here, preferred_element_type=jnp.float32)
        * scaling
        + pos_bias
    )
    key_mask = usable[:, None, None, :]
    local_top = jnp.max(jnp.where(key_mask, scores, neg_big), axis=-1)
    weights = jnp.where(key_mask, jnp.exp(scores - local_top[..., None]), 0.0)
    local_total = jnp.sum(weights, axis=-1)
    local_sum = jnp.einsum(
        "rshk,khd->rshd",
        weights.astype(jnp.bfloat16),
        values_here,
        preferred_element_type=jnp.float32,
    )
    global_top = lax.pmax(local_top, "seq")
    factor = jnp.exp(local_top - global_top)
    cache_total, cache_sum = lax.psum((local_total * factor, local_sum * factor[..., None]), "seq")
    fresh_k = new_k.reshape(req_count, step_count, head_count, head_size)
    fresh_v = new_v.reshape(req_count, step_count, head_count, head_size)
    step_ids = jnp.arange(step_count, dtype=jnp.int32)
    step_gap = step_ids[:, None] - step_ids[None, :]
    fresh_bucket = rel_bucket[jnp.clip(step_gap, 0, dist_limit - 1)]
    fresh_hot = (fresh_bucket[..., None] == jnp.arange(bucket_count, dtype=jnp.int32)).astype(
        jnp.float32
    )
    fresh_bias = jnp.einsum("stb,bh->sht", fresh_hot, bias_table, precision=lax.Precision.HIGHEST)
    fresh_scores = (
        jnp.einsum("rshd,rthd->rsht", queries, fresh_k, preferred_element_type=jnp.float32)
        * scaling
        + fresh_bias[None]
    )
    causal = (step_gap >= 0)[None, :, None, :]
    fresh_top = jnp.max(jnp.where(causal, fresh_scores, neg_big), axis=-1)
    overall = jnp.maximum(global_top, fresh_top)
    fresh_weights = jnp.where(causal, jnp.exp(fresh_scores - overall[..., None]), 0.0)
    rescale = jnp.exp(global_top - overall)
    weight_total = cache_total * rescale + jnp.sum(fresh_weights, axis=-1)
    value_sum = cache_sum * rescale[..., None] + jnp.einsum(
        "rsht,rthd->rshd",
        fresh_weights.astype(jnp.bfloat16),
        fresh_v,
        preferred_element_type=jnp.float32,
    )
    attended = (
        (value_sum / weight_total[..., None])
        .astype(jnp.bfloat16)
        .reshape(req_count * step_count, model_width)
    )
    attn_flat = jnp.dot(attended, out_proj, preferred_element_type=jnp.float32).astype(jnp.bfloat16)
    attn_out = attn_flat.reshape(req_count, step_count, local_width)
    residual = hidden_in.astype(jnp.float32) + attn_out.astype(jnp.float32)
    gained = residual * norm_gain
    partial_logits = jnp.dot(
        gained.reshape(-1, local_width), router_w, precision=lax.Precision.HIGHEST
    )
    square_sum, logit_sum = lax.psum((jnp.sum(residual * residual, axis=-1), partial_logits), "seq")
    inverse = lax.rsqrt(square_sum / model_width + eps_norm)
    normed = (gained * inverse[..., None]).astype(jnp.bfloat16).reshape(-1, local_width)
    logits = logit_sum * inverse.reshape(-1)[:, None]
    chosen_ids = expert_ids.reshape(-1, top_count)
    chosen = jnp.take_along_axis(logits, chosen_ids, axis=1)
    mix_weight = jnp.stack(
        [jax.nn.sigmoid(chosen[:, 0] - chosen[:, 1]), jax.nn.sigmoid(chosen[:, 1] - chosen[:, 0])],
        axis=1,
    )
    flat_ids = chosen_ids.reshape(-1)
    expert_hit = (flat_ids[:, None] == jnp.arange(expert_total, dtype=jnp.int32)[None, :]).astype(
        jnp.int32
    )
    slot_rank = jnp.sum((jnp.cumsum(expert_hit, axis=0) - expert_hit) * expert_hit, axis=1)
    dest_row = flat_ids * MOST + slot_rank
    route_rows = (
        dest_row[:, None] == jnp.arange(expert_total * MOST, dtype=jnp.int32)[None, :]
    ).astype(jnp.bfloat16)
    token_rows = jnp.repeat(normed, top_count, axis=0)
    outgoing = jnp.einsum(
        "as,ad->sd", route_rows, token_rows, preferred_element_type=jnp.float32
    ).astype(jnp.bfloat16)
    outgoing = outgoing.reshape(lax.axis_size("expert"), expert_here, MOST, normed.shape[1])
    full_rows = lax.all_gather(
        lax.all_to_all(outgoing, "expert", split_axis=0, concat_axis=0, tiled=True),
        "seq",
        axis=3,
        tiled=True,
    )
    preact = jnp.einsum("aemd,edgf->aemgf", full_rows, w_in, preferred_element_type=jnp.float32)
    hidden = (jax.nn.gelu(preact[..., 0, :]) * preact[..., 1, :]).astype(jnp.bfloat16)
    partial_out = jnp.einsum("aemf,efd->aemd", hidden, w_down, preferred_element_type=jnp.float32)
    processed = lax.psum_scatter(partial_out, "seq", scatter_dimension=3, tiled=True).astype(
        jnp.bfloat16
    )
    returned_rows = lax.all_to_all(processed, "expert", split_axis=0, concat_axis=0, tiled=True)
    gathered = jnp.einsum(
        "as,sd->ad",
        route_rows,
        returned_rows.reshape(-1, local_width),
        preferred_element_type=jnp.float32,
    )
    mixed_sum = jnp.sum(
        gathered.reshape(-1, top_count, local_width) * mix_weight[..., None], axis=1
    )
    moe_out = mixed_sum.astype(jnp.bfloat16).reshape(req_count, step_count, local_width)
    return (attn_out, moe_out)


def solution(mesh):
    return jax.shard_map(
        body,
        mesh=mesh,
        in_specs=(
            P("expert", None, None),
            P("expert", None, None),
            P("expert", None, None),
            P("expert", "seq", None, None),
            P("expert", "seq", None, None),
            P("expert"),
            P("expert"),
            P("expert", None),
            P("expert", None),
            P(),
            P(),
            P("expert", None, "seq"),
            P(None, "seq"),
            P("seq"),
            P("seq", None),
            P("expert", None, None),
            P("expert", None, None, "seq"),
            P("expert", "seq", None),
        ),
        out_specs=(P("expert", None, "seq"), P("expert", None, "seq")),
        check_vma=False,
    )
```

profile of v0, /device:TPU:1, one launch (start us, length us, event | category | flops | bytes accessed | tf_op | source)
XLA Modules:
  0.0 1109.0 jit_solution(15222342766936235365)
XLA Ops:
  8.0 0.8 multiply_reduce_fusion.1
  8.7 0.8 pad_add_fusion
  10.0 0.7 iota_add_fusion
  10.8 0.7 bitcast_and_fusion
  11.6 1.5 gather_fusion.1
  13.4 90.5 %gather_fusion = s32[16384]{0:T(1024)S(1)} fusion(s32[16388]{0:T(1024)S(1)} %copy-done.1, s32[16384]{0:T(1024)S(1)} %broadcast_clamp_fusion), kind=kCustom, calls=%fused_computation | custom fusion | bytes 196608 | tf_op jit(solution)/shard_map/gather | solution.py:67
  104.6 0.9 copy.200
  105.8 0.8 fusion.2
  106.5 0.8 copy.191
  107.7 1.8 select_reduce_fusion
  109.6 247.4 %pmax.7 = f32[8,4,16]{2,0,1:T(8,128)S(1)} all-reduce(f32[8,4,16]{2,0,1:T(8,128)S(1)} %copy.196), channel_id=1, replica_groups=mesh['seq'=64,'expert'=8] {'seq'}, use_global_device_ids=true, to_apply=%region_4.5 | all-reduce | flops 512 | bytes 4096 | tf_op jit(solution)/shard_map/pmax | solution.py:89
  357.4 0.9 select_reduce_fusion.1
  359.7 1.7 copy.194
  361.9 1.9 fusion.5
  363.8 0.8 copy.214
  365.1 1.0 reshape.277
  366.1 0.9 fusion.39
  367.0 246.2 %psum.29 = f32[8,4,16]{2,0,1:T(8,128)S(1)} all-reduce(f32[8,4,16]{2,0,1:T(8,128)} %get-tuple-element.10), channel_id=1, replica_groups=mesh['seq'=64,'expert'=8] {'seq'}, use_global_device_ids=true, to_apply=%region_8.9 | all-reduce | flops 512 | bytes 4096 | tf_op jit(solution)/shard_map/psum | solution.py:91
  614.5 0.8 copy.213
  615.5 1.2 fusion.21
  617.5 246.1 %all-reduce = (f32[8,4]{1,0:T(8,128)S(1)}, f32[32,16]{0,1:T(8,128)S(1)}) all-reduce(f32[8,4]{1,0:T(8,128)S(1)} %get-tuple-element.14, f32[32,16]{0,1:T(8,128)S(1)} %fusion.65), channel_id=1, replica_groups=mesh['seq'=64,'expert'=8] {'seq'}, use_global_device_ids=true, to_apply=%region_13.14 | all-reduce | flops 544 | bytes 4352 | tf_op jit(solution)/shard_map/psum | solution.py:130
  864.8 9.8 all-to-all-start
  875.1 5.9 all-to-all-done
  881.2 56.9 %all_gather.3 = bf16[8,2,8,1024]{2,0,1,3:T(8,128)(2,1)S(1)} all-gather(bf16[8,2,8,16]{2,0,1,3:T(8,128)(2,1)S(1)} %copy.217), channel_id=1, replica_groups=mesh['seq'=64,'expert'=8] {'seq'}, dimensions={3}, use_global_device_ids=true | all-gather | bytes 266240 | tf_op jit(solution)/shard_map/all_gather | solution.py:154
  938.1 1.2 fusion.6
  939.6 6.0 copy.242
  945.5 7.1 reshape.320
  952.7 0.8 gather_fusion.2
  953.7 132.3 %reduce-scatter.4.cloned.1.call-done = f32[16,128]{1,0:T(8,128)} async-done(((f32[1024,128]{1,0:T(8,128)}), f32[16,128]{1,0:T(8,128)}) %reduce-scatter.4.cloned.1.call-update) | async-done | bytes 8208
  1086.0 0.8 reshape.321
  1087.6 7.0 all-to-all-start.1
  1094.7 6.4 all-to-all-done.1
  (113 shorter events, 12.0 us)
Async XLA Ops:
  7.2 930.9 %copy-start = (bf16[2,1024,2,44]{1,2,3,0:T(2,128)(2,1)S(1)}, bf16[2,1024,2,44]{1,2,3,0:T(2,128)(2,1)}, u32[]{:S(2)}) copy-start(bf16[2,1024,2,44]{1,2,3,0:T(2,128)(2,1)} %param.34) | copy-start | bytes 1081348
  7.2 6.2 copy-start.1
  7.2 608.4 %all-reduce.3.cloned.1.call-start = ((), (), s32[]{:S(2)}) async-start(), calls=%async_computation.3 | async-start | bytes 524288 | tf_op jit(solution)/shard_map/psum | solution.py:91
  7.3 350.2 %copy-start.15 = (pred[4,4]{1,0:T(4,128)(4,1)}, pred[4,4]{1,0:T(4,128)(4,1)S(1)}, u32[]{:S(2)}) copy-start(pred[4,4]{1,0:T(4,128)(4,1)S(1)} %subtract_compare_fusion) | copy-start | bytes 52
  11.5 345.4 %copy-start.8 = (pred[8,512]{1,0:T(8,128)(4,1)}, pred[8,512]{1,0:T(8,128)(4,1)S(1)}, u32[]{:S(2)}) copy-start(pred[8,512]{1,0:T(8,128)(4,1)S(1)} %bitcast_and_fusion) | copy-start | bytes 12292
  13.4 90.6 %copy-start.6 = (bf16[8,4,1024]{2,1,0:T(4,128)(2,1)S(1)}, bf16[8,4,1024]{2,1,0:T(4,128)(2,1)}, u32[]{:S(2)}) copy-start(bf16[8,4,1024]{2,1,0:T(4,128)(2,1)} %param.18) | copy-start | bytes 196612
  13.4 90.8 %copy-start.7 = (bf16[8,4,1024]{2,1,0:T(4,128)(2,1)S(1)}, bf16[8,4,1024]{2,1,0:T(4,128)(2,1)}, u32[]{:S(2)}) copy-start(bf16[8,4,1024]{2,1,0:T(4,128)(2,1)} %param.19) | copy-start | bytes 196612
  13.4 92.1 %copy-start.12 = (f32[32,16]{0,1:T(8,128)S(1)}, f32[32,16]{0,1:T(8,128)}, u32[]{:S(2)}) copy-start(f32[32,16]{0,1:T(8,128)} %param.28) | copy-start | bytes 6148
  13.4 93.1 %copy-start.2 = (bf16[1,4,128,1024]{3,2,1,0:T(8,128)(2,1)S(1)}, bf16[1,4,128,1024]{3,2,1,0:T(8,128)(2,1)}, u32[]{:S(2)}) copy-start(bf16[1,4,128,1024]{3,2,1,0:T(8,128)(2,1)} %param.21) | copy-start | bytes 3145732
  104.2 1.6 copy-start.3
  105.7 251.7 %copy-start.11 = (f32[4,16,4]{1,2,0:T(4,128)}, f32[4,16,4]{1,2,0:T(4,128)S(1)}, u32[]{:S(2)}) copy-start(f32[4,16,4]{1,2,0:T(4,128)S(1)} %convolution_bitcast_fusion.2) | copy-start | bytes 3076
  357.0 2.0 copy-start.5
  361.8 255.1 %copy-start.9 = (bf16[1024,16]{0,1:T(8,128)(2,1)S(1)}, bf16[1024,16]{0,1:T(8,128)(2,1)}, u32[]{:S(2)}) copy-start(bf16[1024,16]{0,1:T(8,128)(2,1)} %param.30) | copy-start | bytes 98308
  361.8 255.4 %copy-start.13 = (bf16[8,4,16]{2,1,0:T(4,128)(2,1)S(1)}, bf16[8,4,16]{2,1,0:T(4,128)(2,1)}, u32[]{:S(2)}) copy-start(bf16[8,4,16]{2,1,0:T(4,128)(2,1)} %param.29) | copy-start | bytes 3076
  361.8 255.4 %copy-start.16 = (f32[16]{0:T(128)S(1)}, f32[16]{0:T(128)}, u32[]{:S(2)}) copy-start(f32[16]{0:T(128)} %param.31) | copy-start | bytes 196
  361.8 255.4 %copy-start.14 = (f32[16,16]{1,0:T(8,128)S(1)}, f32[16,16]{1,0:T(8,128)}, u32[]{:S(2)}) copy-start(f32[16,16]{1,0:T(8,128)} %param.32) | copy-start | bytes 3076
  617.2 322.1 %copy-start.10 = (bf16[32,16]{1,0:T(8,128)(2,1)}, bf16[32,16]{1,0:T(8,128)(2,1)S(1)}, u32[]{:S(2)}) copy-start(bf16[32,16]{1,0:T(8,128)(2,1)S(1)} %copy.212) | copy-start | bytes 3076
  864.8 16.2 %all-to-all-start = ((bf16[8,2,128]{2,1,0:T(2,128)(2,1)}), bf16[8,2,128]{2,1,0:T(2,128)(2,1)S(1)}, u32[]{:S(2)}, u32[]{:S(2)}) async-start(bf16[8,2,128]{2,1,0:T(2,128)(2,1)} %reshape.322), calls=%async_computation | async-start | bytes 8192 | tf_op jit(solution)/shard_map/all_to_all | solution.py:155
  874.5 211.5 %reduce-scatter.4.cloned.1.call-start = ((), (), s32[]{:S(2)}) async-start(), calls=%async_computation.4 | async-start | bytes 532480
  881.2 58.1 %copy-start.4 = (bf16[2,44,1024]{2,0,1:T(2,128)(2,1)S(1)}, bf16[2,44,1024]{2,0,1:T(2,128)(2,1)}, u32[]{:S(2)}) copy-start(bf16[2,44,1024]{2,0,1:T(2,128)(2,1)} %param.35) | copy-start | bytes 540676
  1087.6 13.5 %all-to-all-start.1 = ((bf16[8,2,128]{2,1,0:T(2,128)(2,1)}), bf16[8,2,128]{2,1,0:T(2,128)(2,1)S(1)}, u32[]{:S(2)}, u32[]{:S(2)}) async-start(bf16[8,2,128]{2,1,0:T(2,128)(2,1)} %reshape.324), calls=%async_computation.1 | async-start | bytes 8192 | tf_op jit(solution)/shard_map/all_to_all | solution.py:166
Sparse Core Ops, SparseCore 0:
  363.9 188.2 all-reduce.2
  952.7 133.2 reduce-scatter.3
where the time goes:
time: 1120 us; the launch traced here: 1110 us
  blocking collectives  797 us (71%)
  waiting for transfers between devices  145 us (13%)
  local copies, waits for them, and re-layouts  119 us (11%)
  starting transfers between devices  16.9 us (2%)
  between operations  14.6 us (1%)
    pmax x1, blocking collectives, body(): global_top = lax.pmax(local_top, 'seq')  247 us
    psum x1, blocking collectives, body(): lax.psum((local_total * factor, local_sum * factor[..., None]), 'seq')  246 us
    psum x1, blocking collectives, body(): lax.psum((jnp.sum(residual * residual, axis=-1), partial_logits), 'seq')  246 us
    unnamed x3, waiting for transfers between devices  132 us
    gather x2, local copies, waits for them, and re-layouts, body(): buckets = rel_bucket[distance]  90.6 us
    all_gather x1, blocking collectives, body(): lax.all_gather(lax.all_to_all(outgoing, 'expert', split_axis=0, concat_ax...  56.9 us
  transfers between devices with their start and end apart: 4, of which 3 were waited for; matrix products, arithmetic and copies ran while one was open for 1% of the time, Pallas kernels for 0%

commit v1 on v0

v1 whole, which is shorter than its diff:
```python
import math

import jax
import jax.numpy as jnp
from jax import lax
from jax.sharding import PartitionSpec as P

MOST = 8
neg_big = -1e30
eps_norm = 1e-06
f32 = jnp.float32
bf16 = jnp.bfloat16


def short(x):
    return lax.reduce_precision(x, 8, 7)


def two_parts(x):
    high = short(x)
    return high, short(x - high)


def body(
    new_q,
    new_k,
    new_v,
    k_cache,
    v_cache,
    lengths,
    prompt_group,
    prefix_table,
    page_table,
    rel_bucket,
    bias_table,
    hidden_in,
    out_proj,
    norm_gain,
    router_w,
    expert_ids,
    w_in,
    w_down,
):
    reqs, steps, width = new_q.shape
    bucket_count, heads = bias_table.shape
    head_size = width // heads
    pages_here, page_len = k_cache.shape[1:3]
    group_rows = prefix_table.shape[0]
    expert_here = w_in.shape[0]
    local = out_proj.shape[1]
    top = expert_ids.shape[2]
    seq_size = lax.axis_size("seq")
    owners = lax.axis_size("expert")
    seq_index = lax.axis_index("seq")
    pool_index = lax.axis_index("expert")
    tokens = reqs * steps
    slots = expert_here * MOST
    rows = owners * slots
    pairs = heads // 2
    lanes = 2 * head_size
    scaling = 1.0 / math.sqrt(head_size)

    with jax.named_scope("positions"):
        local_group = prompt_group - pool_index * group_rows
        prefix_rows = jnp.where(
            (local_group == 0)[:, None], prefix_table[0][None], prefix_table[1][None]
        )
        full_table = jnp.concatenate([prefix_rows, page_table], axis=1)
        page_ids = seq_index * pages_here + jnp.arange(pages_here, dtype=jnp.int32)
        matches = full_table[:, None, :] == page_ids[None, :, None]
        spots = jnp.arange(full_table.shape[1], dtype=jnp.int32)
        logical = jnp.max(jnp.where(matches, spots, -1), axis=2)
        within = jnp.arange(page_len, dtype=jnp.int32)
        key_grid = logical[:, :, None] * page_len + within
        usable = (logical[:, :, None] >= 0) & (key_grid < lengths[:, None, None])
        key_pos = key_grid.reshape(reqs, -1)
        usable = usable.reshape(reqs, -1)
        query_pos = lengths[:, None] + jnp.arange(steps, dtype=jnp.int32)
        distance = query_pos[:, :, None] - key_pos[:, None, :]
        names = jnp.arange(bucket_count + 1, dtype=jnp.int32)
        first_at = jnp.sum((rel_bucket[None, :] < names[:, None]).astype(jnp.int32), axis=1)
        opens = first_at[:-1][:, None, None, None]
        closes = first_at[1:][:, None, None, None]
        onehot = ((distance >= opens) & (distance < closes)).astype(f32)
        pos_bias = jnp.einsum("brsk,bh->hrsk", onehot, bias_table, precision=lax.Precision.HIGHEST)

    with jax.named_scope("local_attention"):
        queries = new_q.reshape(reqs, steps, heads, head_size)
        keys_here = k_cache[0].reshape(-1, heads, head_size)
        values_here = v_cache[0].reshape(-1, heads, head_size)
        scores = jnp.einsum("rshd,khd->hrsk", queries, keys_here, preferred_element_type=f32)
        scores = jnp.where(usable[None, :, None, :], scores * scaling + pos_bias, neg_big)
        part_top = short(jnp.max(scores, axis=-1))
        weights = jnp.where(
            usable[None, :, None, :], jnp.exp(scores - part_top[..., None]), 0.0
        )
        part_total = jnp.sum(weights, axis=-1)
        part_sum = jnp.einsum(
            "hrsk,khd->hrsd", weights.astype(bf16), values_here, preferred_element_type=f32
        )
        total_high, total_low = two_parts(part_total)
        stacked = jnp.stack(
            [part_top, total_high, total_low, jnp.zeros_like(part_top)], axis=-1
        )
        extra = jnp.repeat(stacked.astype(bf16), head_size // 4, axis=-1)
        both = jnp.concatenate([part_sum.astype(bf16), extra], axis=2)
        both = both.reshape(pairs, 2, reqs, 2 * steps, head_size)
        outgoing = jnp.transpose(both, (0, 2, 3, 1, 4)).reshape(seq_size, 2 * steps, lanes)

    with jax.named_scope("exchange_parts"):
        parts = lax.all_to_all(outgoing, "seq", split_axis=0, concat_axis=0, tiled=True)

    with jax.named_scope("combine_parts"):
        my_pair = seq_index // reqs
        my_req = seq_index % reqs
        lane = jnp.arange(lanes, dtype=jnp.int32)
        lane_head = lane // head_size
        quarter = head_size // 4
        from_top = (lane[:, None] == lane_head[None, :] * head_size).astype(bf16)
        from_high = lane[:, None] == lane_head[None, :] * head_size + quarter
        from_low = lane[:, None] == lane_head[None, :] * head_size + 2 * quarter
        from_total = (from_high | from_low).astype(bf16)
        sums = parts[:, :steps].astype(f32)
        extras = parts[:, steps:].reshape(seq_size * steps, lanes)
        tops = jnp.dot(extras, from_top, preferred_element_type=f32)
        totals = jnp.dot(extras, from_total, preferred_element_type=f32)
        tops = tops.reshape(seq_size, steps, lanes)
        totals = totals.reshape(seq_size, steps, lanes)

        def mine(x):
            return lax.dynamic_slice(
                x, (my_req, 0, my_pair * lanes), (1, steps, lanes)
            )[0].astype(f32)

        fresh_q, fresh_k, fresh_v = mine(new_q), mine(new_k), mine(new_v)
        same_head = (lane_head[:, None] == lane_head[None, :]).astype(f32)
        products = fresh_q[:, None, :] * fresh_k[None, :, :]
        fresh_scores = jnp.dot(
            products.reshape(steps * steps, lanes), same_head, precision=lax.Precision.HIGHEST
        ).reshape(steps, steps, lanes)
        near_bias = lax.dynamic_slice(bias_table, (0, my_pair * 2), (steps, 2))
        near_bias = jnp.repeat(near_bias, head_size, axis=1)
        step_ids = jnp.arange(steps, dtype=jnp.int32)
        gap = step_ids[:, None] - step_ids[None, :]
        fresh_bias = sum(
            jnp.where((gap == g)[..., None], near_bias[g], 0.0) for g in range(steps)
        )
        causal = (gap >= 0)[..., None]
        fresh_scores = jnp.where(causal, fresh_scores * scaling + fresh_bias, neg_big)
        peak = jnp.maximum(jnp.max(tops, axis=0), jnp.max(fresh_scores, axis=1))
        factor = jnp.exp(tops - peak)
        fresh_weights = jnp.where(causal, jnp.exp(fresh_scores - peak[:, None, :]), 0.0)
        total = jnp.sum(totals * factor, axis=0) + jnp.sum(fresh_weights, axis=1)
        value_sum = jnp.sum(sums * factor, axis=0) + jnp.sum(
            short(fresh_weights) * fresh_v[None], axis=1
        )
        attended = (value_sum / total).astype(bf16)

    with jax.named_scope("share_attended"):
        shared = jnp.broadcast_to(attended[None], (seq_size, steps, lanes))
        heard = lax.all_to_all(shared, "seq", split_axis=0, concat_axis=0, tiled=True)

    with jax.named_scope("project"):
        heard = heard.reshape(pairs, tokens, lanes)
        attn_flat = jnp.einsum(
            "ptd,pdn->tn",
            heard,
            out_proj.reshape(pairs, lanes, local),
            preferred_element_type=f32,
        ).astype(bf16)
        attn_out = attn_flat.reshape(reqs, steps, local)
        residual = hidden_in.reshape(tokens, local).astype(f32) + attn_flat.astype(f32)
        gained = residual * norm_gain
        squares = jnp.sum(residual * residual, axis=1)
        part_logits = jnp.dot(gained, router_w, precision=lax.Precision.HIGHEST)

    with jax.named_scope("route"):
        chosen_ids = expert_ids.reshape(tokens, top)
        total_experts = owners * expert_here
        expert_names = jnp.arange(total_experts, dtype=jnp.int32)
        flat_ids = chosen_ids.reshape(-1)
        expert_hit = (flat_ids[:, None] == expert_names[None, :]).astype(jnp.int32)
        order = jnp.arange(tokens * top, dtype=jnp.int32)
        earlier = (order[:, None] > order[None, :]) & (flat_ids[:, None] == flat_ids[None, :])
        slot_rank = jnp.sum(earlier.astype(jnp.int32), axis=1)
        dest_row = flat_ids * MOST + slot_rank
        route = (
            dest_row[None, :] == jnp.arange(rows, dtype=jnp.int32)[:, None]
        ).astype(bf16)
        signed_hit = (
            (chosen_ids[:, :1] == expert_names).astype(f32)
            - (chosen_ids[:, 1:] == expert_names).astype(f32)
        )
        lead = jnp.sum(part_logits * signed_hit, axis=1)
        square_high, square_low = two_parts(squares)
        lead_high, lead_low = two_parts(lead)
        ones = jnp.ones_like(lead)
        sides = []
        for sign in (ones, -ones):
            sides.append(
                jnp.concatenate(
                    [
                        gained,
                        jnp.stack(
                            [square_high, square_low, sign * lead_high, sign * lead_low], axis=1
                        ),
                    ],
                    axis=1,
                ).astype(bf16)
            )
        token_rows = jnp.stack(sides, axis=1).reshape(tokens * top, local + 4)
        sent = jnp.dot(route, token_rows, preferred_element_type=f32).astype(bf16)

    with jax.named_scope("to_owners"):
        sent = sent.reshape(owners, slots, local + 4)
        got = lax.all_to_all(sent, "expert", split_axis=0, concat_axis=0, tiled=True)

    with jax.named_scope("share_rows"):
        turned = jnp.pad(got.reshape(rows, local + 4).T, ((0, 4), (0, 0)))
        shared_rows = jnp.broadcast_to(turned[None], (seq_size, local + 8, rows))
        all_rows = lax.all_to_all(shared_rows, "seq", split_axis=0, concat_axis=0, tiled=True)

    with jax.named_scope("experts"):
        features = all_rows[:, :local].reshape(width, rows)
        sides = jnp.sum(all_rows[:, local : local + 4].astype(f32), axis=0)
        inverse = lax.rsqrt((sides[0] + sides[1]) / width + eps_norm)
        mix = jax.nn.sigmoid((sides[2] + sides[3]) * inverse)
        preact = jnp.einsum("edgf,dr->egfr", w_in, features, preferred_element_type=f32) * inverse
        owner_of = jnp.arange(rows, dtype=jnp.int32) // MOST % expert_here
        here = owner_of[None, :] == jnp.arange(expert_here, dtype=jnp.int32)[:, None]
        hidden = jax.nn.gelu(preact[:, 0]) * preact[:, 1]
        hidden = jnp.where(here[:, None, :], hidden, 0.0).astype(bf16)
        part_out = jnp.einsum("efd,efr->dr", w_down, hidden, preferred_element_type=f32)
        part_out = (part_out * mix).astype(bf16).reshape(seq_size, local, rows)

    with jax.named_scope("sum_hidden_units"):
        pieces = lax.all_to_all(part_out, "seq", split_axis=0, concat_axis=0, tiled=True)
        processed = jnp.sum(pieces.astype(f32), axis=0).astype(bf16)

    with jax.named_scope("to_tokens"):
        back = processed.T.reshape(owners, slots, local)
        returned = lax.all_to_all(back, "expert", split_axis=0, concat_axis=0, tiled=True)
        token_route = jnp.sum(route.reshape(rows, tokens, top), axis=2)
        moe_out = jnp.einsum(
            "rt,rd->td", token_route, returned.reshape(rows, local), preferred_element_type=f32
        )
        moe_out = moe_out.astype(bf16).reshape(reqs, steps, local)
    return (attn_out, moe_out)


def solution(mesh):
    return jax.shard_map(
        body,
        mesh=mesh,
        in_specs=(
            P("expert", None, None),
            P("expert", None, None),
            P("expert", None, None),
            P("expert", "seq", None, None),
            P("expert", "seq", None, None),
            P("expert"),
            P("expert"),
            P("expert", None),
            P("expert", None),
            P(),
            P(),
            P("expert", None, "seq"),
            P(None, "seq"),
            P("seq"),
            P("seq", None),
            P("expert", None, None),
            P("expert", None, None, "seq"),
            P("expert", "seq", None),
        ),
        out_specs=(P("expert", None, "seq"), P("expert", None, "seq")),
        check_vma=False,
    )
```

time: 1120 us -> 127 us (0.11)
  blocking collectives: 797 us -> 16.4 us
  local copies, waits for them, and re-layouts: 119 us -> 16 us
  waiting for transfers between devices: 145 us -> 49 us
  starting transfers between devices: 16.9 us -> 32.2 us
  between operations: 14.6 us -> 1.12 us
    psum x2 -> x0, blocking collectives: 492 us -> none  [the longest x1 246 us: body(): lax.psum((local_total * factor, local_sum * factor[..., None]), 'seq')]
    pmax x1 -> x0, blocking collectives: 247 us -> none  [body(): global_top = lax.pmax(local_top, 'seq')]
    unnamed x3 -> x0, waiting for transfers between devices: 132 us -> none
    gather x9 -> x0, local copies, waits for them, and re-layouts: 93.4 us -> none  [the longest x2 90.6 us: body(): buckets = rel_bucket[distance]]
    all_gather x1 -> x0, blocking collectives: 56.9 us -> none  [body(): lax.all_gather(lax.all_to_all(outgoing, 'expert', split_axis=0, concat_ax...]
    all_to_all x2 -> x5, waiting for transfers between devices: 12.4 us -> 49 us  [the longest x1 14.7 us: body(): lax.all_to_all(shared_rows, 'seq', split_axis=0, concat_axis=0, tiled=True)]
    all_to_all x0 -> x1, blocking collectives: none -> 16.4 us  [body(): lax.all_to_all(sent, 'expert', split_axis=0, concat_axis=0, tiled=True)]
    all_to_all x2 -> x5, starting transfers between devices: 16.8 us -> 32.2 us  [the longest x1 11.8 us: body(): lax.all_to_all(outgoing, 'seq', split_axis=0, concat_axis=0, tiled=True)]
  transfers between devices with their start and end apart: 4 -> 5, of which waited for: 3 -> 5; matrix products, arithmetic and copies ran while one was open for 1% -> 3% of each run, Pallas kernels for 0% -> 0%
where the time goes in v1:
time: 127 us; the launch traced here: 126 us
  waiting for transfers between devices  49 us (39%)
  starting transfers between devices  32.2 us (25%)
  blocking collectives  16.4 us (13%)
  local copies, waits for them, and re-layouts  16 us (13%)
  other arithmetic  7.27 us (6%)
  matrix products  4.04 us (3%)
    all_to_all x1, blocking collectives, body(): lax.all_to_all(sent, 'expert', split_axis=0, concat_axis=0, tiled=True)  16.4 us
    all_to_all x1, waiting for transfers between devices, body(): lax.all_to_all(shared_rows, 'seq', split_axis=0, concat_axis=0, tiled=True)  14.7 us
    all_to_all x1, waiting for transfers between devices, body(): lax.all_to_all(part_out, 'seq', split_axis=0, concat_axis=0, tiled=True)  11.8 us
    all_to_all x1, starting transfers between devices, body(): lax.all_to_all(outgoing, 'seq', split_axis=0, concat_axis=0, tiled=True)  11.8 us
    all_to_all x1, waiting for transfers between devices, body(): lax.all_to_all(shared, 'seq', split_axis=0, concat_axis=0, tiled=True)  9.77 us
    all_to_all x1, waiting for transfers between devices, body(): lax.all_to_all(outgoing, 'seq', split_axis=0, concat_axis=0, tiled=True)  7.13 us
    all_to_all x1, starting transfers between devices, body(): lax.all_to_all(part_out, 'seq', split_axis=0, concat_axis=0, tiled=True)  6.21 us
    all_to_all x1, starting transfers between devices, body(): lax.all_to_all(shared_rows, 'seq', split_axis=0, concat_axis=0, tiled=True)  6.02 us
  transfers between devices with their start and end apart: 5, of which 5 were waited for; matrix products, arithmetic and copies ran while one was open for 3% of the time, Pallas kernels for 0%

profile of v1, /device:TPU:1, one launch (start us, length us, event | category | flops | bytes accessed | tf_op | source)
XLA Modules:
  0.0 126.0 jit_solution(11475244528574194584)
XLA Ops:
  0.7 0.8 slice_bitcast_fusion.5
  1.4 0.7 subtract_compare_fusion
  2.2 0.8 pad_add_fusion
  3.2 0.7 iota_add_fusion
  4.0 0.7 bitcast_and_fusion
  4.7 1.3 %convert_reduce_fusion = s32[33]{0:T(128)S(1)} fusion(s32[16388]{0:T(1024)} %param.27), kind=kLoop, calls=%fused_computation | loop fusion | flops 1622379 | bytes 65684 | tf_op jit(solution)/shard_map/positions/reduce_sum | solution.py:81
  6.0 1.7 %copy.104 = bf16[1,4,128,1024]{2,1,3,0:T(4,128)(2,1)S(1)} copy(bf16[1,4,128,1024]{3,2,1,0:T(8,128)(2,1)} %param.21) | data formatting | bytes 2097152 | tf_op args[3]
  8.8 0.9 fusion
  9.8 0.9 fusion.97
  11.7 0.6 broadcast_in_dim.222
  12.3 0.9 concatenate.49
  13.2 1.7 %copy.107 = bf16[1,4,128,1024]{2,1,3,0:T(4,128)(2,1)S(1)} copy(bf16[1,4,128,1024]{3,2,1,0:T(8,128)(2,1)} %param.22) | data formatting | bytes 2097152 | tf_op args[4]
  16.6 0.8 reshape.582
  17.4 11.8 %all-to-all-start = ((bf16[64,8,128]{2,1,0:T(8,128)(2,1)}), bf16[64,8,128]{2,1,0:T(8,128)(2,1)S(1)}, u32[]{:S(2)}, u32[]{:S(2)}) async-start(bf16[64,8,128]{2,1,0:T(8,128)(2,1)} %reshape.582), calls=%async_computation | async-start | bytes 262144 | tf_op jit(solution)/shard_map/exchange_parts/all_to_all | solution.py:111
  30.1 0.7 bitcast_convert_fusion.2
  30.8 0.7 bitcast_convert_fusion
  32.4 7.1 %all-to-all-done = bf16[64,8,128]{2,1,0:T(8,128)(2,1)S(1)} async-done(((bf16[64,8,128]{2,1,0:T(8,128)(2,1)}), bf16[64,8,128]{2,1,0:T(8,128)(2,1)S(1)}, u32[]{:S(2)}, u32[]{:S(2)}) %all-to-all-start) | async-done | bytes 131104 | tf_op jit(solution)/shard_map/exchange_parts/all_to_all | solution.py:111
  40.1 0.6 broadcast_in_dim.242
  40.8 4.9 %all-to-all-start.1 = ((bf16[64,4,128]{2,1,0:T(4,128)(2,1)}), bf16[64,4,128]{2,1,0:T(4,128)(2,1)S(1)}, u32[]{:S(2)}, u32[]{:S(2)}) async-start(bf16[64,4,128]{2,1,0:T(4,128)(2,1)} %broadcast_in_dim.242), calls=%async_computation.1 | async-start | bytes 131072 | tf_op jit(solution)/shard_map/share_attended/all_to_all | solution.py:161
  45.7 9.8 %all-to-all-done.1 = bf16[64,4,128]{2,1,0:T(4,128)(2,1)S(1)} async-done(((bf16[64,4,128]{2,1,0:T(4,128)(2,1)}), bf16[64,4,128]{2,1,0:T(4,128)(2,1)S(1)}, u32[]{:S(2)}, u32[]{:S(2)}) %all-to-all-start.1) | async-done | bytes 65568 | tf_op jit(solution)/shard_map/share_attended/all_to_all | solution.py:161
  56.6 16.4 %all_to_all.30 = bf16[8,2,160]{2,1,0:T(2,128)(2,1)S(1)} all-to-all(bf16[8,2,160]{2,1,0:T(2,128)(2,1)S(1)} %reshape.618), channel_id=1, replica_groups=mesh['seq'=64,'expert'=8] {'expert'}, dimensions={0} | all-to-all | bytes 10240 | tf_op jit(solution)/shard_map/to_owners/all_to_all | solution.py:216
  73.2 0.8 broadcast_in_dim.244
  74.0 6.0 %all-to-all-start.3 = ((bf16[64,24,128]{2,1,0:T(8,128)(2,1)}), bf16[64,24,128]{2,1,0:T(8,128)(2,1)S(1)}, u32[]{:S(2)}, u32[]{:S(2)}) async-start(bf16[64,24,128]{2,1,0:T(8,128)(2,1)} %broadcast_in_dim.244), calls=%async_computation.3 | async-start | bytes 786432 | tf_op jit(solution)/shard_map/share_rows/all_to_all | solution.py:221
  80.0 14.7 %all-to-all-done.3 = bf16[64,24,128]{2,1,0:T(8,128)(2,1)S(1)} async-done(((bf16[64,24,128]{2,1,0:T(8,128)(2,1)}), bf16[64,24,128]{2,1,0:T(8,128)(2,1)S(1)}, u32[]{:S(2)}, u32[]{:S(2)}) %all-to-all-start.3) | async-done | bytes 393248 | tf_op jit(solution)/shard_map/share_rows/all_to_all | solution.py:221
  95.4 0.8 copy.124
  96.3 6.2 %all-to-all-start.4 = ((bf16[64,16,128]{2,1,0:T(8,128)(2,1)}), bf16[64,16,128]{2,1,0:T(8,128)(2,1)S(1)}, u32[]{:S(2)}, u32[]{:S(2)}) async-start(bf16[64,16,128]{2,1,0:T(8,128)(2,1)} %bitcast.49), calls=%async_computation.4 | async-start | bytes 524288 | tf_op jit(solution)/shard_map/sum_hidden_units/all_to_all | solution.py:237
  102.7 11.8 %all-to-all-done.4 = bf16[64,16,128]{2,1,0:T(8,128)(2,1)S(1)} async-done(((bf16[64,16,128]{2,1,0:T(8,128)(2,1)}), bf16[64,16,128]{2,1,0:T(8,128)(2,1)S(1)}, u32[]{:S(2)}, u32[]{:S(2)}) %all-to-all-start.4) | async-done | bytes 262176 | tf_op jit(solution)/shard_map/sum_hidden_units/all_to_all | solution.py:237
  114.7 0.7 reshape.620
  115.3 3.3 %all-to-all-start.5 = ((bf16[8,2,128]{2,1,0:T(2,128)(2,1)}), bf16[8,2,128]{2,1,0:T(2,128)(2,1)S(1)}, u32[]{:S(2)}, u32[]{:S(2)}) async-start(bf16[8,2,128]{2,1,0:T(2,128)(2,1)} %reshape.620), calls=%async_computation.5 | async-start | bytes 8192 | tf_op jit(solution)/shard_map/to_tokens/all_to_all | solution.py:242
  118.7 0.7 copy.113
  119.4 5.6 %all-to-all-done.5 = bf16[8,2,128]{2,1,0:T(2,128)(2,1)S(1)} async-done(((bf16[8,2,128]{2,1,0:T(2,128)(2,1)}), bf16[8,2,128]{2,1,0:T(2,128)(2,1)S(1)}, u32[]{:S(2)}, u32[]{:S(2)}) %all-to-all-start.5) | async-done | bytes 4128 | tf_op jit(solution)/shard_map/to_tokens/all_to_all | solution.py:242
  125.4 0.7 copy.127
  (106 shorter events, 9.2 us)
Async XLA Ops:
  0.6 94.2 %copy-start = (bf16[2,1024,2,44]{1,2,3,0:T(2,128)(2,1)S(1)}, bf16[2,1024,2,44]{1,2,3,0:T(2,128)(2,1)}, u32[]{:S(2)}) copy-start(bf16[2,1024,2,44]{1,2,3,0:T(2,128)(2,1)} %param.34) | copy-start | bytes 1081348
  7.8 0.8 copy-start.3
  7.8 1.1 copy-start.8
  15.4 0.9 copy-start.1
  15.9 13.4 %copy-start.5 = (s32[8,4,2]{0,2,1:T(2,128)S(1)}, s32[8,4,2]{0,2,1:T(2,128)}, u32[]{:S(2)}) copy-start(s32[8,4,2]{0,2,1:T(2,128)} %param.33) | copy-start | bytes 772
  15.9 16.2 %copy-start.6 = (bf16[8,4,16]{2,1,0:T(4,128)(2,1)S(1)}, bf16[8,4,16]{2,1,0:T(4,128)(2,1)}, u32[]{:S(2)}) copy-start(bf16[8,4,16]{2,1,0:T(4,128)(2,1)} %param.29) | copy-start | bytes 3076
  17.4 38.0 %copy-start.4 = (bf16[1024,16]{0,1:T(8,128)(2,1)S(1)}, bf16[1024,16]{0,1:T(8,128)(2,1)}, u32[]{:S(2)}) copy-start(bf16[1024,16]{0,1:T(8,128)(2,1)} %param.30) | copy-start | bytes 98308
  17.4 38.1 %copy-start.7 = (f32[16]{0:T(128)S(1)}, f32[16]{0:T(128)}, u32[]{:S(2)}) copy-start(f32[16]{0:T(128)} %param.31) | copy-start | bytes 196
  17.4 38.2 %copy-start.9 = (f32[16,16]{1,0:T(8,128)S(1)}, f32[16,16]{1,0:T(8,128)}, u32[]{:S(2)}) copy-start(f32[16,16]{1,0:T(8,128)} %param.32) | copy-start | bytes 3076
  17.4 22.1 %all-to-all-start = ((bf16[64,8,128]{2,1,0:T(8,128)(2,1)}), bf16[64,8,128]{2,1,0:T(8,128)(2,1)S(1)}, u32[]{:S(2)}, u32[]{:S(2)}) async-start(bf16[64,8,128]{2,1,0:T(8,128)(2,1)} %reshape.582), calls=%async_computation | async-start | bytes 262144 | tf_op jit(solution)/shard_map/exchange_parts/all_to_all | solution.py:111
  40.8 14.7 %all-to-all-start.1 = ((bf16[64,4,128]{2,1,0:T(4,128)(2,1)}), bf16[64,4,128]{2,1,0:T(4,128)(2,1)S(1)}, u32[]{:S(2)}, u32[]{:S(2)}) async-start(bf16[64,4,128]{2,1,0:T(4,128)(2,1)} %broadcast_in_dim.242), calls=%async_computation.1 | async-start | bytes 131072 | tf_op jit(solution)/shard_map/share_attended/all_to_all | solution.py:161
  74.0 21.2 %copy-start.2 = (bf16[2,44,1024]{2,0,1:T(2,128)(2,1)S(1)}, bf16[2,44,1024]{2,0,1:T(2,128)(2,1)}, u32[]{:S(2)}) copy-start(bf16[2,44,1024]{2,0,1:T(2,128)(2,1)} %param.35) | copy-start | bytes 540676
  74.0 20.7 %all-to-all-start.3 = ((bf16[64,24,128]{2,1,0:T(8,128)(2,1)}), bf16[64,24,128]{2,1,0:T(8,128)(2,1)S(1)}, u32[]{:S(2)}, u32[]{:S(2)}) async-start(bf16[64,24,128]{2,1,0:T(8,128)(2,1)} %broadcast_in_dim.244), calls=%async_computation.3 | async-start | bytes 786432 | tf_op jit(solution)/shard_map/share_rows/all_to_all | solution.py:221
  96.3 18.2 %all-to-all-start.4 = ((bf16[64,16,128]{2,1,0:T(8,128)(2,1)}), bf16[64,16,128]{2,1,0:T(8,128)(2,1)S(1)}, u32[]{:S(2)}, u32[]{:S(2)}) async-start(bf16[64,16,128]{2,1,0:T(8,128)(2,1)} %bitcast.49), calls=%async_computation.4 | async-start | bytes 524288 | tf_op jit(solution)/shard_map/sum_hidden_units/all_to_all | solution.py:237
  115.3 9.7 %all-to-all-start.5 = ((bf16[8,2,128]{2,1,0:T(2,128)(2,1)}), bf16[8,2,128]{2,1,0:T(2,128)(2,1)S(1)}, u32[]{:S(2)}, u32[]{:S(2)}) async-start(bf16[8,2,128]{2,1,0:T(2,128)(2,1)} %reshape.620), calls=%async_computation.5 | async-start | bytes 8192 | tf_op jit(solution)/shard_map/to_tokens/all_to_all | solution.py:242

commit v2 on v1

--- a/solution.py
+++ b/solution.py
@@ -184,6 +184,7 @@
         earlier = (order[:, None] > order[None, :]) & (flat_ids[:, None] == flat_ids[None, :])
         slot_rank = jnp.sum(earlier.astype(jnp.int32), axis=1)
         dest_row = flat_ids * MOST + slot_rank
+        dest_pair = dest_row.reshape(tokens, top)
         route = (
             dest_row[None, :] == jnp.arange(rows, dtype=jnp.int32)[:, None]
         ).astype(bf16)
@@ -204,19 +205,26 @@
                         jnp.stack(
                             [square_high, square_low, sign * lead_high, sign * lead_low], axis=1
                         ),
+                        jnp.zeros((tokens, lanes - local - 4), f32),
                     ],
                     axis=1,
                 ).astype(bf16)
             )
-        token_rows = jnp.stack(sides, axis=1).reshape(tokens * top, local + 4)
+        token_rows = jnp.stack(sides, axis=1).reshape(tokens * top, lanes)
         sent = jnp.dot(route, token_rows, preferred_element_type=f32).astype(bf16)
 
     with jax.named_scope("to_owners"):
-        sent = sent.reshape(owners, slots, local + 4)
+        sent = sent.reshape(owners, slots, lanes)
+        sent, first_rows, second_rows = lax.optimization_barrier(
+            (sent, dest_pair[:, 0], dest_pair[:, 1])
+        )
         got = lax.all_to_all(sent, "expert", split_axis=0, concat_axis=0, tiled=True)
+        row_names = jnp.arange(rows, dtype=jnp.int32)[:, None]
+        first_route = (row_names == first_rows[None, :]).astype(bf16)
+        got, first_route = lax.optimization_barrier((got, first_route))
 
     with jax.named_scope("share_rows"):
-        turned = jnp.pad(got.reshape(rows, local + 4).T, ((0, 4), (0, 0)))
+        turned = got.reshape(rows, lanes)[:, : local + 8].T
         shared_rows = jnp.broadcast_to(turned[None], (seq_size, local + 8, rows))
         all_rows = lax.all_to_all(shared_rows, "seq", split_axis=0, concat_axis=0, tiled=True)
 
@@ -234,13 +242,15 @@
         part_out = (part_out * mix).astype(bf16).reshape(seq_size, local, rows)
 
     with jax.named_scope("sum_hidden_units"):
+        part_out, second_rows = lax.optimization_barrier((part_out, second_rows))
         pieces = lax.all_to_all(part_out, "seq", split_axis=0, concat_axis=0, tiled=True)
+        token_route = first_route + (row_names == second_rows[None, :]).astype(bf16)
+        pieces, token_route = lax.optimization_barrier((pieces, token_route))
         processed = jnp.sum(pieces.astype(f32), axis=0).astype(bf16)
 
     with jax.named_scope("to_tokens"):
         back = processed.T.reshape(owners, slots, local)
         returned = lax.all_to_all(back, "expert", split_axis=0, concat_axis=0, tiled=True)
-        token_route = jnp.sum(route.reshape(rows, tokens, top), axis=2)
         moe_out = jnp.einsum(
             "rt,rd->td", token_route, returned.reshape(rows, local), preferred_element_type=f32
         )

time: 127 us -> 129 us (1.016)
  blocking collectives: 16.4 us -> 0 us
  starting transfers between devices: 32.2 us -> 42.1 us
  waiting for transfers between devices: 49 us -> 56 us
    all_to_all x1 -> x0, blocking collectives: 16.4 us -> none  [body(): lax.all_to_all(sent, 'expert', split_axis=0, concat_axis=0, tiled=True)]
    all_to_all x0 -> x1, starting transfers between devices: none -> 10 us  [body(): lax.all_to_all(sent, 'expert', split_axis=0, concat_axis=0, tiled=True)]
    all_to_all x0 -> x1, waiting for transfers between devices: none -> 6.95 us  [body(): lax.all_to_all(sent, 'expert', split_axis=0, concat_axis=0, tiled=True)]
    unnamed x28 -> x26, local copies, waits for them, and re-layouts: 5.4 us -> 5.19 us
  transfers between devices with their start and end apart: 5 -> 6, of which waited for: 5 -> 6; matrix products, arithmetic and copies ran while one was open for 3% -> 3% of each run, Pallas kernels for 0% -> 0%
where the time goes in v2:
time: 129 us; the launch traced here: 128 us
  waiting for transfers between devices  56 us (43%)
  starting transfers between devices  42.1 us (33%)
  local copies, waits for them, and re-layouts  16.8 us (13%)
  other arithmetic  7.26 us (6%)
  matrix products  4.6 us (4%)
    all_to_all x1, waiting for transfers between devices, body(): lax.all_to_all(shared_rows, 'seq', split_axis=0, concat_axis=0, tiled=True)  14.7 us
    all_to_all x1, waiting for transfers between devices, body(): lax.all_to_all(part_out, 'seq', split_axis=0, concat_axis=0, tiled=True)  12 us
    all_to_all x1, starting transfers between devices, body(): lax.all_to_all(outgoing, 'seq', split_axis=0, concat_axis=0, tiled=True)  11.8 us
    all_to_all x1, starting transfers between devices, body(): lax.all_to_all(sent, 'expert', split_axis=0, concat_axis=0, tiled=True)  10 us
    all_to_all x1, waiting for transfers between devices, body(): lax.all_to_all(shared, 'seq', split_axis=0, concat_axis=0, tiled=True)  9.77 us
    all_to_all x1, waiting for transfers between devices, body(): lax.all_to_all(sent, 'expert', split_axis=0, concat_axis=0, tiled=True)  6.95 us
    all_to_all x1, waiting for transfers between devices, body(): lax.all_to_all(outgoing, 'seq', split_axis=0, concat_axis=0, tiled=True)  6.92 us
    all_to_all x1, starting transfers between devices, body(): lax.all_to_all(part_out, 'seq', split_axis=0, concat_axis=0, tiled=True)  6.2 us
  transfers between devices with their start and end apart: 6, of which 6 were waited for; matrix products, arithmetic and copies ran while one was open for 3% of the time, Pallas kernels for 0%

profile of v2, /device:TPU:1, one launch (start us, length us, event | category | flops | bytes accessed | tf_op | source)
XLA Modules:
  0.0 127.9 jit_solution(10484434105526898090)
XLA Ops:
  0.7 0.8 slice_bitcast_fusion.8
  1.4 0.7 subtract_compare_fusion
  2.2 0.8 pad_add_fusion
  3.2 0.7 iota_add_fusion
  4.0 0.7 bitcast_and_fusion
  4.7 1.3 convert_reduce_fusion
  6.0 1.7 %copy.137 = bf16[1,4,128,1024]{2,1,3,0:T(4,128)(2,1)S(1)} copy(bf16[1,4,128,1024]{3,2,1,0:T(8,128)(2,1)} %param.21) | data formatting | bytes 2097152 | tf_op args[3]
  8.8 0.9 fusion
  9.8 0.9 fusion.98
  12.3 0.9 concatenate.51
  13.2 1.7 %copy.140 = bf16[1,4,128,1024]{2,1,3,0:T(4,128)(2,1)S(1)} copy(bf16[1,4,128,1024]{3,2,1,0:T(8,128)(2,1)} %param.22) | data formatting | bytes 2097152 | tf_op args[4]
  16.6 0.8 reshape.592
  17.4 11.8 %all-to-all-start = ((bf16[64,8,128]{2,1,0:T(8,128)(2,1)}), bf16[64,8,128]{2,1,0:T(8,128)(2,1)S(1)}, u32[]{:S(2)}, u32[]{:S(2)}) async-start(bf16[64,8,128]{2,1,0:T(8,128)(2,1)} %reshape.592), calls=%async_computation | async-start | bytes 262144 | tf_op jit(solution)/shard_map/exchange_parts/all_to_all | solution.py:111
  30.3 0.7 bitcast_convert_fusion.2
  31.0 0.7 bitcast_convert_fusion
  32.6 6.9 %all-to-all-done = bf16[64,8,128]{2,1,0:T(8,128)(2,1)S(1)} async-done(((bf16[64,8,128]{2,1,0:T(8,128)(2,1)}), bf16[64,8,128]{2,1,0:T(8,128)(2,1)S(1)}, u32[]{:S(2)}, u32[]{:S(2)}) %all-to-all-start) | async-done | bytes 131104 | tf_op jit(solution)/shard_map/exchange_parts/all_to_all | solution.py:111
  40.8 4.9 %all-to-all-start.1 = ((bf16[64,4,128]{2,1,0:T(4,128)(2,1)}), bf16[64,4,128]{2,1,0:T(4,128)(2,1)S(1)}, u32[]{:S(2)}, u32[]{:S(2)}) async-start(bf16[64,4,128]{2,1,0:T(4,128)(2,1)} %broadcast_in_dim.245), calls=%async_computation.1 | async-start | bytes 131072 | tf_op jit(solution)/shard_map/share_attended/all_to_all | solution.py:161
  45.7 9.8 %all-to-all-done.1 = bf16[64,4,128]{2,1,0:T(4,128)(2,1)S(1)} async-done(((bf16[64,4,128]{2,1,0:T(4,128)(2,1)}), bf16[64,4,128]{2,1,0:T(4,128)(2,1)S(1)}, u32[]{:S(2)}, u32[]{:S(2)}) %all-to-all-start.1) | async-done | bytes 65568 | tf_op jit(solution)/shard_map/share_attended/all_to_all | solution.py:161
  57.3 0.7 convolution_convert_fusion.1
  58.0 10.0 %all-to-all-start.2 = ((bf16[8,16,128]{2,1,0:T(8,128)(2,1)}), bf16[8,16,128]{2,1,0:T(8,128)(2,1)S(1)}, u32[]{:S(2)}, u32[]{:S(2)}) async-start(bf16[8,16,128]{2,1,0:T(8,128)(2,1)} %bitcast.36), calls=%async_computation.2 | async-start | bytes 65536 | tf_op jit(solution)/shard_map/to_owners/all_to_all | solution.py:221
  68.1 7.0 %all-to-all-done.2 = bf16[8,16,128]{2,1,0:T(8,128)(2,1)S(1)} async-done(((bf16[8,16,128]{2,1,0:T(8,128)(2,1)}), bf16[8,16,128]{2,1,0:T(8,128)(2,1)S(1)}, u32[]{:S(2)}, u32[]{:S(2)}) %all-to-all-start.2) | async-done | bytes 32800 | tf_op jit(solution)/shard_map/to_owners/all_to_all | solution.py:221
  75.1 0.8 broadcast_in_dim.247
  75.9 5.9 %all-to-all-start.3 = ((bf16[64,24,128]{2,1,0:T(8,128)(2,1)}), bf16[64,24,128]{2,1,0:T(8,128)(2,1)S(1)}, u32[]{:S(2)}, u32[]{:S(2)}) async-start(bf16[64,24,128]{2,1,0:T(8,128)(2,1)} %broadcast_in_dim.247), calls=%async_computation.3 | async-start | bytes 786432 | tf_op jit(solution)/shard_map/share_rows/all_to_all | solution.py:229
  81.9 14.7 %all-to-all-done.3 = bf16[64,24,128]{2,1,0:T(8,128)(2,1)S(1)} async-done(((bf16[64,24,128]{2,1,0:T(8,128)(2,1)}), bf16[64,24,128]{2,1,0:T(8,128)(2,1)S(1)}, u32[]{:S(2)}, u32[]{:S(2)}) %all-to-all-start.3) | async-done | bytes 393248 | tf_op jit(solution)/shard_map/share_rows/all_to_all | solution.py:229
  97.3 0.8 copy.165
  98.1 6.2 %all-to-all-start.4 = ((bf16[64,16,128]{2,1,0:T(8,128)(2,1)}), bf16[64,16,128]{2,1,0:T(8,128)(2,1)S(1)}, u32[]{:S(2)}, u32[]{:S(2)}) async-start(bf16[64,16,128]{2,1,0:T(8,128)(2,1)} %bitcast.51), calls=%async_computation.4 | async-start | bytes 524288 | tf_op jit(solution)/shard_map/sum_hidden_units/all_to_all | solution.py:246
  104.4 12.0 %all-to-all-done.4 = bf16[64,16,128]{2,1,0:T(8,128)(2,1)S(1)} async-done(((bf16[64,16,128]{2,1,0:T(8,128)(2,1)}), bf16[64,16,128]{2,1,0:T(8,128)(2,1)S(1)}, u32[]{:S(2)}, u32[]{:S(2)}) %all-to-all-start.4) | async-done | bytes 262176 | tf_op jit(solution)/shard_map/sum_hidden_units/all_to_all | solution.py:246
  116.5 0.7 reshape.629
  117.2 3.3 %all-to-all-start.5 = ((bf16[8,2,128]{2,1,0:T(2,128)(2,1)}), bf16[8,2,128]{2,1,0:T(2,128)(2,1)S(1)}, u32[]{:S(2)}, u32[]{:S(2)}) async-start(bf16[8,2,128]{2,1,0:T(2,128)(2,1)} %reshape.629), calls=%async_computation.5 | async-start | bytes 8192 | tf_op jit(solution)/shard_map/to_tokens/all_to_all | solution.py:253
  120.5 0.7 copy.146
  121.2 5.7 %all-to-all-done.5 = bf16[8,2,128]{2,1,0:T(2,128)(2,1)S(1)} async-done(((bf16[8,2,128]{2,1,0:T(2,128)(2,1)}), bf16[8,2,128]{2,1,0:T(2,128)(2,1)S(1)}, u32[]{:S(2)}, u32[]{:S(2)}) %all-to-all-start.5) | async-done | bytes 4128 | tf_op jit(solution)/shard_map/to_tokens/all_to_all | solution.py:253
  127.2 0.7 copy.168
  (113 shorter events, 11.0 us)
Async XLA Ops:
  0.6 96.1 %copy-start = (bf16[2,1024,2,44]{1,2,3,0:T(2,128)(2,1)S(1)}, bf16[2,1024,2,44]{1,2,3,0:T(2,128)(2,1)}, u32[]{:S(2)}) copy-start(bf16[2,1024,2,44]{1,2,3,0:T(2,128)(2,1)} %param.34) | copy-start | bytes 1081348
  7.8 0.8 copy-start.3
  7.8 1.1 copy-start.8
  15.4 0.9 copy-start.1
  15.9 13.4 %copy-start.5 = (s32[8,4,2]{0,2,1:T(2,128)S(1)}, s32[8,4,2]{0,2,1:T(2,128)}, u32[]{:S(2)}) copy-start(s32[8,4,2]{0,2,1:T(2,128)} %param.33) | copy-start | bytes 772
  15.9 16.4 %copy-start.6 = (bf16[8,4,16]{2,1,0:T(4,128)(2,1)S(1)}, bf16[8,4,16]{2,1,0:T(4,128)(2,1)}, u32[]{:S(2)}) copy-start(bf16[8,4,16]{2,1,0:T(4,128)(2,1)} %param.29) | copy-start | bytes 3076
  17.4 38.0 %copy-start.4 = (bf16[1024,16]{0,1:T(8,128)(2,1)S(1)}, bf16[1024,16]{0,1:T(8,128)(2,1)}, u32[]{:S(2)}) copy-start(bf16[1024,16]{0,1:T(8,128)(2,1)} %param.30) | copy-start | bytes 98308
  17.4 38.1 %copy-start.7 = (f32[16]{0:T(128)S(1)}, f32[16]{0:T(128)}, u32[]{:S(2)}) copy-start(f32[16]{0:T(128)} %param.31) | copy-start | bytes 196
  17.4 38.2 %copy-start.9 = (f32[16,16]{1,0:T(8,128)S(1)}, f32[16,16]{1,0:T(8,128)}, u32[]{:S(2)}) copy-start(f32[16,16]{1,0:T(8,128)} %param.32) | copy-start | bytes 3076
  17.4 22.1 %all-to-all-start = ((bf16[64,8,128]{2,1,0:T(8,128)(2,1)}), bf16[64,8,128]{2,1,0:T(8,128)(2,1)S(1)}, u32[]{:S(2)}, u32[]{:S(2)}) async-start(bf16[64,8,128]{2,1,0:T(8,128)(2,1)} %reshape.592), calls=%async_computation | async-start | bytes 262144 | tf_op jit(solution)/shard_map/exchange_parts/all_to_all | solution.py:111
  40.8 14.7 %all-to-all-start.1 = ((bf16[64,4,128]{2,1,0:T(4,128)(2,1)}), bf16[64,4,128]{2,1,0:T(4,128)(2,1)S(1)}, u32[]{:S(2)}, u32[]{:S(2)}) async-start(bf16[64,4,128]{2,1,0:T(4,128)(2,1)} %broadcast_in_dim.245), calls=%async_computation.1 | async-start | bytes 131072 | tf_op jit(solution)/shard_map/share_attended/all_to_all | solution.py:161
  58.0 17.0 %all-to-all-start.2 = ((bf16[8,16,128]{2,1,0:T(8,128)(2,1)}), bf16[8,16,128]{2,1,0:T(8,128)(2,1)S(1)}, u32[]{:S(2)}, u32[]{:S(2)}) async-start(bf16[8,16,128]{2,1,0:T(8,128)(2,1)} %bitcast.36), calls=%async_computation.2 | async-start | bytes 65536 | tf_op jit(solution)/shard_map/to_owners/all_to_all | solution.py:221
  75.9 21.1 %copy-start.2 = (bf16[2,44,1024]{2,0,1:T(2,128)(2,1)S(1)}, bf16[2,44,1024]{2,0,1:T(2,128)(2,1)}, u32[]{:S(2)}) copy-start(bf16[2,44,1024]{2,0,1:T(2,128)(2,1)} %param.35) | copy-start | bytes 540676
  75.9 20.7 %all-to-all-start.3 = ((bf16[64,24,128]{2,1,0:T(8,128)(2,1)}), bf16[64,24,128]{2,1,0:T(8,128)(2,1)S(1)}, u32[]{:S(2)}, u32[]{:S(2)}) async-start(bf16[64,24,128]{2,1,0:T(8,128)(2,1)} %broadcast_in_dim.247), calls=%async_computation.3 | async-start | bytes 786432 | tf_op jit(solution)/shard_map/share_rows/all_to_all | solution.py:229
  98.1 18.2 %all-to-all-start.4 = ((bf16[64,16,128]{2,1,0:T(8,128)(2,1)}), bf16[64,16,128]{2,1,0:T(8,128)(2,1)S(1)}, u32[]{:S(2)}, u32[]{:S(2)}) async-start(bf16[64,16,128]{2,1,0:T(8,128)(2,1)} %bitcast.51), calls=%async_computation.4 | async-start | bytes 524288 | tf_op jit(solution)/shard_map/sum_hidden_units/all_to_all | solution.py:246
  117.2 9.7 %all-to-all-start.5 = ((bf16[8,2,128]{2,1,0:T(2,128)(2,1)}), bf16[8,2,128]{2,1,0:T(2,128)(2,1)S(1)}, u32[]{:S(2)}, u32[]{:S(2)}) async-start(bf16[8,2,128]{2,1,0:T(2,128)(2,1)} %reshape.629), calls=%async_computation.5 | async-start | bytes 8192 | tf_op jit(solution)/shard_map/to_tokens/all_to_all | solution.py:253

commit v3 on v1

--- a/solution.py
+++ b/solution.py
@@ -85,27 +85,35 @@
         pos_bias = jnp.einsum("brsk,bh->hrsk", onehot, bias_table, precision=lax.Precision.HIGHEST)
 
     with jax.named_scope("local_attention"):
-        queries = new_q.reshape(reqs, steps, heads, head_size)
-        keys_here = k_cache[0].reshape(-1, heads, head_size)
-        values_here = v_cache[0].reshape(-1, heads, head_size)
-        scores = jnp.einsum("rshd,khd->hrsk", queries, keys_here, preferred_element_type=f32)
-        scores = jnp.where(usable[None, :, None, :], scores * scaling + pos_bias, neg_big)
-        part_top = short(jnp.max(scores, axis=-1))
-        weights = jnp.where(
-            usable[None, :, None, :], jnp.exp(scores - part_top[..., None]), 0.0
-        )
-        part_total = jnp.sum(weights, axis=-1)
+        pair_lane = jnp.arange(lanes, dtype=jnp.int32)
+        in_second = pair_lane >= head_size
+        own_lane = in_second[None, :] == (jnp.arange(2) == 1)[:, None]
+        queries = jnp.transpose(new_q.reshape(tokens, pairs, lanes), (1, 0, 2))
+        queries = jnp.where(own_lane[None, :, None, :], queries[:, None], 0).astype(bf16)
+        queries = queries.reshape(pairs, 2, reqs, steps, lanes)
+        keys_here = k_cache[0].reshape(-1, pairs, lanes)
+        values_here = v_cache[0].reshape(-1, pairs, lanes)
+        allowed = usable[None, None, :, None, :]
+        scores = jnp.einsum("pgrsd,kpd->pgrsk", queries, keys_here, preferred_element_type=f32)
+        pair_bias = pos_bias.reshape(pairs, 2, reqs, steps, -1)
+        scores = jnp.where(allowed, scores * scaling + pair_bias, neg_big)
+        part_top = short(jnp.max(scores, axis=-1, keepdims=True))
+        weights = jnp.where(allowed, jnp.exp(scores - part_top), 0.0)
+        part_total = jnp.sum(weights, axis=-1, keepdims=True)
         part_sum = jnp.einsum(
-            "hrsk,khd->hrsd", weights.astype(bf16), values_here, preferred_element_type=f32
+            "pgrsk,kpd->pgrsd", weights.astype(bf16), values_here, preferred_element_type=f32
         )
         total_high, total_low = two_parts(part_total)
-        stacked = jnp.stack(
-            [part_top, total_high, total_low, jnp.zeros_like(part_top)], axis=-1
-        )
-        extra = jnp.repeat(stacked.astype(bf16), head_size // 4, axis=-1)
-        both = jnp.concatenate([part_sum.astype(bf16), extra], axis=2)
-        both = both.reshape(pairs, 2, reqs, 2 * steps, head_size)
-        outgoing = jnp.transpose(both, (0, 2, 3, 1, 4)).reshape(seq_size, 2 * steps, lanes)
+        spot = pair_lane % head_size // (head_size // 4)
+        extra = jnp.where(
+            spot == 0,
+            part_top,
+            jnp.where(spot == 1, total_high, jnp.where(spot == 2, total_low, 0.0)),
+        )
+        mine_sum = jnp.where(in_second, part_sum[:, 1], part_sum[:, 0]).astype(bf16)
+        mine_extra = jnp.where(in_second, extra[:, 1], extra[:, 0]).astype(bf16)
+        outgoing = jnp.concatenate([mine_sum, mine_extra], axis=-1)
+        outgoing = outgoing.reshape(seq_size, steps, 2 * lanes)
 
     with jax.named_scope("exchange_parts"):
         parts = lax.all_to_all(outgoing, "seq", split_axis=0, concat_axis=0, tiled=True)
@@ -120,8 +128,8 @@
         from_high = lane[:, None] == lane_head[None, :] * head_size + quarter
         from_low = lane[:, None] == lane_head[None, :] * head_size + 2 * quarter
         from_total = (from_high | from_low).astype(bf16)
-        sums = parts[:, :steps].astype(f32)
-        extras = parts[:, steps:].reshape(seq_size * steps, lanes)
+        sums = parts[:, :, :lanes].astype(f32)
+        extras = parts[:, :, lanes:].reshape(seq_size * steps, lanes)
         tops = jnp.dot(extras, from_top, preferred_element_type=f32)
         totals = jnp.dot(extras, from_total, preferred_element_type=f32)
         tops = tops.reshape(seq_size, steps, lanes)

time: 127 us -> 123 us (0.969)
  local copies, waits for them, and re-layouts: 16 us -> 12.3 us
    unnamed x28, local copies, waits for them, and re-layouts: 5.4 us -> 3.71 us
where the time goes in v3:
time: 123 us; the launch traced here: 122 us
  waiting for transfers between devices  49 us (40%)
  starting transfers between devices  32.2 us (26%)
  blocking collectives  16.4 us (13%)
  local copies, waits for them, and re-layouts  12.3 us (10%)
  other arithmetic  6.87 us (6%)
  matrix products  4.42 us (4%)
    all_to_all x1, blocking collectives, body(): lax.all_to_all(sent, 'expert', split_axis=0, concat_axis=0, tiled=True)  16.4 us
    all_to_all x1, waiting for transfers between devices, body(): lax.all_to_all(shared_rows, 'seq', split_axis=0, concat_axis=0, tiled=True)  14.7 us
    all_to_all x1, waiting for transfers between devices, body(): lax.all_to_all(part_out, 'seq', split_axis=0, concat_axis=0, tiled=True)  11.8 us
    all_to_all x1, starting transfers between devices, body(): lax.all_to_all(outgoing, 'seq', split_axis=0, concat_axis=0, tiled=True)  11.8 us
    all_to_all x1, waiting for transfers between devices, body(): lax.all_to_all(shared, 'seq', split_axis=0, concat_axis=0, tiled=True)  9.77 us
    all_to_all x1, waiting for transfers between devices, body(): lax.all_to_all(outgoing, 'seq', split_axis=0, concat_axis=0, tiled=True)  7.1 us
    all_to_all x1, starting transfers between devices, body(): lax.all_to_all(part_out, 'seq', split_axis=0, concat_axis=0, tiled=True)  6.2 us
    all_to_all x1, starting transfers between devices, body(): lax.all_to_all(shared_rows, 'seq', split_axis=0, concat_axis=0, tiled=True)  6.02 us
  transfers between devices with their start and end apart: 5, of which 5 were waited for; matrix products, arithmetic and copies ran while one was open for 3% of the time, Pallas kernels for 0%

profile of v3, /device:TPU:1, one launch (start us, length us, event | category | flops | bytes accessed | tf_op | source)
XLA Modules:
  0.0 122.3 jit_solution(3764447250918495095)
XLA Ops:
  0.7 0.8 slice_bitcast_fusion.7
  1.4 0.7 subtract_compare_fusion
  2.2 0.8 pad_add_fusion
  3.2 0.7 iota_add_fusion
  4.0 0.7 bitcast_and_fusion
  4.8 1.3 %convert_reduce_fusion = s32[33]{0:T(128)S(1)} fusion(s32[16388]{0:T(1024)} %param.27), kind=kLoop, calls=%fused_computation | loop fusion | flops 1622379 | bytes 65684 | tf_op jit(solution)/shard_map/positions/reduce_sum | solution.py:81
  6.2 1.6 %fusion.4 = f32[16,8,4,512]{3,0,2,1:T(8,128)S(1)} fusion(s32[8,4,512]{2,1,0:T(4,128)S(1)} %broadcast_subtract_fusion, s32[32]{0:T(128)S(1)} %get-tuple-element.33, s32[32]{0:T(128)S(1)} %get-tuple-element.32, f32[32,16]{0,1:T(8,128)} %param.28), kind=kOutput, calls=%fused_computation.6 | convolution fusion | flops 102236160 | bytes 1116416 | tf_op jit(solution)/shard_map/positions/brsk,bh->hrsk/dot_general | solution.py:85
  7.8 0.6 copy.142
  8.4 0.6 copy-done.1
  9.3 0.6 copy-done.4
  10.0 0.6 fusion.107
  11.1 0.8 copy-done.2
  12.9 0.7 copy.149
  13.7 11.8 %all-to-all-start = ((bf16[64,4,256]{2,1,0:T(4,128)(2,1)}), bf16[64,4,256]{2,1,0:T(4,128)(2,1)S(1)}, u32[]{:S(2)}, u32[]{:S(2)}) async-start(bf16[64,4,256]{2,1,0:T(4,128)(2,1)} %copy.149), calls=%async_computation | async-start | bytes 262144 | tf_op jit(solution)/shard_map/exchange_parts/all_to_all | solution.py:119
  25.7 0.7 constant_dynamic-slice_fusion
  27.1 0.7 bitcast_convert_fusion
  28.7 7.1 %all-to-all-done = bf16[64,4,256]{2,1,0:T(4,128)(2,1)S(1)} async-done(((bf16[64,4,256]{2,1,0:T(4,128)(2,1)}), bf16[64,4,256]{2,1,0:T(4,128)(2,1)S(1)}, u32[]{:S(2)}, u32[]{:S(2)}) %all-to-all-start) | async-done | bytes 131104 | tf_op jit(solution)/shard_map/exchange_parts/all_to_all | solution.py:119
  36.4 0.6 broadcast_in_dim.316
  37.0 4.9 %all-to-all-start.1 = ((bf16[64,4,128]{2,1,0:T(4,128)(2,1)}), bf16[64,4,128]{2,1,0:T(4,128)(2,1)S(1)}, u32[]{:S(2)}, u32[]{:S(2)}) async-start(bf16[64,4,128]{2,1,0:T(4,128)(2,1)} %broadcast_in_dim.316), calls=%async_computation.1 | async-start | bytes 131072 | tf_op jit(solution)/shard_map/share_attended/all_to_all | solution.py:169
  41.9 9.8 %all-to-all-done.1 = bf16[64,4,128]{2,1,0:T(4,128)(2,1)S(1)} async-done(((bf16[64,4,128]{2,1,0:T(4,128)(2,1)}), bf16[64,4,128]{2,1,0:T(4,128)(2,1)S(1)}, u32[]{:S(2)}, u32[]{:S(2)}) %all-to-all-start.1) | async-done | bytes 65568 | tf_op jit(solution)/shard_map/share_attended/all_to_all | solution.py:169
  52.8 16.4 %all_to_all.30 = bf16[8,2,160]{2,1,0:T(2,128)(2,1)S(1)} all-to-all(bf16[8,2,160]{2,1,0:T(2,128)(2,1)S(1)} %reshape.642), channel_id=1, replica_groups=mesh['seq'=64,'expert'=8] {'expert'}, dimensions={0} | all-to-all | bytes 10240 | tf_op jit(solution)/shard_map/to_owners/all_to_all | solution.py:224
  69.4 0.8 broadcast_in_dim.318
  70.2 6.0 %all-to-all-start.3 = ((bf16[64,24,128]{2,1,0:T(8,128)(2,1)}), bf16[64,24,128]{2,1,0:T(8,128)(2,1)S(1)}, u32[]{:S(2)}, u32[]{:S(2)}) async-start(bf16[64,24,128]{2,1,0:T(8,128)(2,1)} %broadcast_in_dim.318), calls=%async_computation.3 | async-start | bytes 786432 | tf_op jit(solution)/shard_map/share_rows/all_to_all | solution.py:229
  76.3 14.7 %all-to-all-done.3 = bf16[64,24,128]{2,1,0:T(8,128)(2,1)S(1)} async-done(((bf16[64,24,128]{2,1,0:T(8,128)(2,1)}), bf16[64,24,128]{2,1,0:T(8,128)(2,1)S(1)}, u32[]{:S(2)}, u32[]{:S(2)}) %all-to-all-start.3) | async-done | bytes 393248 | tf_op jit(solution)/shard_map/share_rows/all_to_all | solution.py:229
  91.7 0.8 copy.164
  92.5 6.2 %all-to-all-start.4 = ((bf16[64,16,128]{2,1,0:T(8,128)(2,1)}), bf16[64,16,128]{2,1,0:T(8,128)(2,1)S(1)}, u32[]{:S(2)}, u32[]{:S(2)}) async-start(bf16[64,16,128]{2,1,0:T(8,128)(2,1)} %bitcast.52), calls=%async_computation.4 | async-start | bytes 524288 | tf_op jit(solution)/shard_map/sum_hidden_units/all_to_all | solution.py:245
  98.9 11.8 %all-to-all-done.4 = bf16[64,16,128]{2,1,0:T(8,128)(2,1)S(1)} async-done(((bf16[64,16,128]{2,1,0:T(8,128)(2,1)}), bf16[64,16,128]{2,1,0:T(8,128)(2,1)S(1)}, u32[]{:S(2)}, u32[]{:S(2)}) %all-to-all-start.4) | async-done | bytes 262176 | tf_op jit(solution)/shard_map/sum_hidden_units/all_to_all | solution.py:245
  110.9 0.7 reshape.644
  111.6 3.3 %all-to-all-start.5 = ((bf16[8,2,128]{2,1,0:T(2,128)(2,1)}), bf16[8,2,128]{2,1,0:T(2,128)(2,1)S(1)}, u32[]{:S(2)}, u32[]{:S(2)}) async-start(bf16[8,2,128]{2,1,0:T(2,128)(2,1)} %reshape.644), calls=%async_computation.5 | async-start | bytes 8192 | tf_op jit(solution)/shard_map/to_tokens/all_to_all | solution.py:250
  115.0 0.7 copy.153
  115.7 5.6 %all-to-all-done.5 = bf16[8,2,128]{2,1,0:T(2,128)(2,1)S(1)} async-done(((bf16[8,2,128]{2,1,0:T(2,128)(2,1)}), bf16[8,2,128]{2,1,0:T(2,128)(2,1)S(1)}, u32[]{:S(2)}, u32[]{:S(2)}) %all-to-all-start.5) | async-done | bytes 4128 | tf_op jit(solution)/shard_map/to_tokens/all_to_all | solution.py:250
  121.6 0.7 copy.167
  (109 shorter events, 7.4 us)
Async XLA Ops:
  0.6 90.5 %copy-start = (bf16[2,1024,2,44]{1,2,3,0:T(2,128)(2,1)S(1)}, bf16[2,1024,2,44]{1,2,3,0:T(2,128)(2,1)}, u32[]{:S(2)}) copy-start(bf16[2,1024,2,44]{1,2,3,0:T(2,128)(2,1)} %param.34) | copy-start | bytes 1081348
  7.8 1.2 %copy-start.1 = (bf16[1,4,128,1024]{3,2,1,0:T(8,128)(2,1)S(1)}, bf16[1,4,128,1024]{3,2,1,0:T(8,128)(2,1)}, u32[]{:S(2)}) copy-start(bf16[1,4,128,1024]{3,2,1,0:T(8,128)(2,1)} %param.21) | copy-start | bytes 3145732
  9.0 0.8 copy-start.4
  10.6 1.2 %copy-start.2 = (bf16[1,4,128,1024]{3,2,1,0:T(8,128)(2,1)S(1)}, bf16[1,4,128,1024]{3,2,1,0:T(8,128)(2,1)}, u32[]{:S(2)}) copy-start(bf16[1,4,128,1024]{3,2,1,0:T(8,128)(2,1)} %param.22) | copy-start | bytes 3145732
  12.6 13.0 %copy-start.6 = (s32[8,4,2]{0,2,1:T(2,128)S(1)}, s32[8,4,2]{0,2,1:T(2,128)}, u32[]{:S(2)}) copy-start(s32[8,4,2]{0,2,1:T(2,128)} %param.33) | copy-start | bytes 772
  12.6 15.8 %copy-start.7 = (bf16[8,4,16]{2,1,0:T(4,128)(2,1)S(1)}, bf16[8,4,16]{2,1,0:T(4,128)(2,1)}, u32[]{:S(2)}) copy-start(bf16[8,4,16]{2,1,0:T(4,128)(2,1)} %param.29) | copy-start | bytes 3076
  13.7 38.0 %copy-start.5 = (bf16[1024,16]{0,1:T(8,128)(2,1)S(1)}, bf16[1024,16]{0,1:T(8,128)(2,1)}, u32[]{:S(2)}) copy-start(bf16[1024,16]{0,1:T(8,128)(2,1)} %param.30) | copy-start | bytes 98308
  13.7 38.1 %copy-start.8 = (f32[16]{0:T(128)S(1)}, f32[16]{0:T(128)}, u32[]{:S(2)}) copy-start(f32[16]{0:T(128)} %param.31) | copy-start | bytes 196
  13.7 38.2 %copy-start.9 = (f32[16,16]{1,0:T(8,128)S(1)}, f32[16,16]{1,0:T(8,128)}, u32[]{:S(2)}) copy-start(f32[16,16]{1,0:T(8,128)} %param.32) | copy-start | bytes 3076
  13.7 22.1 %all-to-all-start = ((bf16[64,4,256]{2,1,0:T(4,128)(2,1)}), bf16[64,4,256]{2,1,0:T(4,128)(2,1)S(1)}, u32[]{:S(2)}, u32[]{:S(2)}) async-start(bf16[64,4,256]{2,1,0:T(4,128)(2,1)} %copy.149), calls=%async_computation | async-start | bytes 262144 | tf_op jit(solution)/shard_map/exchange_parts/all_to_all | solution.py:119
  37.0 14.7 %all-to-all-start.1 = ((bf16[64,4,128]{2,1,0:T(4,128)(2,1)}), bf16[64,4,128]{2,1,0:T(4,128)(2,1)S(1)}, u32[]{:S(2)}, u32[]{:S(2)}) async-start(bf16[64,4,128]{2,1,0:T(4,128)(2,1)} %broadcast_in_dim.316), calls=%async_computation.1 | async-start | bytes 131072 | tf_op jit(solution)/shard_map/share_attended/all_to_all | solution.py:169
  70.2 21.2 %copy-start.3 = (bf16[2,44,1024]{2,0,1:T(2,128)(2,1)S(1)}, bf16[2,44,1024]{2,0,1:T(2,128)(2,1)}, u32[]{:S(2)}) copy-start(bf16[2,44,1024]{2,0,1:T(2,128)(2,1)} %param.35) | copy-start | bytes 540676
  70.2 20.7 %all-to-all-start.3 = ((bf16[64,24,128]{2,1,0:T(8,128)(2,1)}), bf16[64,24,128]{2,1,0:T(8,128)(2,1)S(1)}, u32[]{:S(2)}, u32[]{:S(2)}) async-start(bf16[64,24,128]{2,1,0:T(8,128)(2,1)} %broadcast_in_dim.318), calls=%async_computation.3 | async-start | bytes 786432 | tf_op jit(solution)/shard_map/share_rows/all_to_all | solution.py:229
  92.5 18.2 %all-to-all-start.4 = ((bf16[64,16,128]{2,1,0:T(8,128)(2,1)}), bf16[64,16,128]{2,1,0:T(8,128)(2,1)S(1)}, u32[]{:S(2)}, u32[]{:S(2)}) async-start(bf16[64,16,128]{2,1,0:T(8,128)(2,1)} %bitcast.52), calls=%async_computation.4 | async-start | bytes 524288 | tf_op jit(solution)/shard_map/sum_hidden_units/all_to_all | solution.py:245
  111.6 9.7 %all-to-all-start.5 = ((bf16[8,2,128]{2,1,0:T(2,128)(2,1)}), bf16[8,2,128]{2,1,0:T(2,128)(2,1)S(1)}, u32[]{:S(2)}, u32[]{:S(2)}) async-start(bf16[8,2,128]{2,1,0:T(2,128)(2,1)} %reshape.644), calls=%async_computation.5 | async-start | bytes 8192 | tf_op jit(solution)/shard_map/to_tokens/all_to_all | solution.py:250
